TPU v7x, 512 devices: a whole 4x4x16 slice. The times are simulated.
512 devices in a mesh: band: 8 (over y, core), pw: 64 (over z, x).
Axes of the slice: x: 4, y: 4, z: 16, core: 2. Of those that a mesh axis runs over, the one named last changes fastest.
Arguments:
- occupied_bands: float32 [2, 16, 3328, 128], P(None, 'band', 'pw'), may hold values from -0.11742834 to 0.11742834
- iterate: float32 [2, 16, 3328, 128], P(None, 'band', 'pw'), may hold values from -2 to 2
- residual: float32 [2, 16, 3328, 128], P(None, 'band', 'pw'), may hold values from -25 to 25, as said below
- old_direction: float32 [2, 16, 3328, 128], P(None, 'band', 'pw'), may hold values from -25 to 25, as said below
- preconditioner: float32 [16, 3328, 128], P('band', 'pw'), may hold values from 0.1 to 1
- old_norm: float32 [16], P('band'), may hold values from 0.4 to 1.6
- eigenvalues: float32 [16], replicated, may hold values from -2 to -0.3
- band_slot: int32 [16], replicated, may hold values from 0 to 15, each once
- potential: float32 [128, 128, 128], P('pw'), may hold values from 0.2 to 1.5
- column_map: int32 [3328], replicated, may hold values from 0 to 16383, as said below
Outputs:
- new_iterate: float32 [2, 16, 3328, 128], P(None, 'band', 'pw')
- new_residual: float32 [2, 16, 3328, 128], P(None, 'band', 'pw')
- direction: float32 [2, 16, 3328, 128], P(None, 'band', 'pw')
- new_norm: float32 [16], P('band')
- density: float32 [128, 128, 128], P('pw', 'band')
Inputs may be any that keep to these rules, and one draw needn't show every extreme that they name: `residual`: random draw per entry, rough from column to column and frequency to frequency. `old_direction`: random draw per entry, rough from column to column and frequency to frequency. `column_map`: distinct flat indices; every column with signed a^2 + b^2 < 32^2 is present, the remaining columns lie outside that disc; the column of flat index 0 is present. `band_slot`: each global band index appears once.
All inputs are finite; a program needn't handle non-finite values.
Results may differ from a plain program's by a relative error of at most 0.0001.
Values sent between devices are 32-bit elements; how exact they have to be, the bound alone decides.
A program may use at most 64 MiB of HBM per device.

v0:
```python
import math
import jax
import jax.numpy as jnp
from jax import lax
from jax.sharding import PartitionSpec as P

exact_mode = lax.Precision.HIGHEST


def phase_table(grid_len, direction_sign):
    indices = jnp.arange(grid_len, dtype=jnp.int32)
    phases = indices[:, None] * indices[None, :] % grid_len
    angles = phases.astype(jnp.float32) * (2.0 * math.pi / grid_len)
    cosine = jnp.cos(angles)
    sine_part = jnp.sin(angles) * direction_sign
    return jnp.stack([jnp.stack([cosine, sine_part]), jnp.stack([-sine_part, cosine])])


def signed_index(values, grid_len):
    return jnp.where(values < grid_len // 2, values, values - grid_len)


def wave_squares(columns, grid_len):
    wave_x = signed_index(columns // grid_len, grid_len)
    wave_y = signed_index(columns % grid_len, grid_len)
    wave_z = signed_index(jnp.arange(grid_len, dtype=jnp.int32), grid_len)
    return (wave_x * wave_x + wave_y * wave_y)[:, None] + (wave_z * wave_z)[None, :]


def correlation(band_rows, vectors):
    real_part = jnp.einsum("pvck,pnck->vn", band_rows, vectors, precision=exact_mode)
    imag_part = jnp.einsum(
        "vck,nck->vn", band_rows[0], vectors[1], precision=exact_mode
    ) - jnp.einsum("vck,nck->vn", band_rows[1], vectors[0], precision=exact_mode)
    return jnp.stack([real_part, imag_part])


def expand(band_rows, weights):
    real_part = jnp.einsum(
        "vck,vn->nck", band_rows[0], weights[0], precision=exact_mode
    ) - jnp.einsum("vck,vn->nck", band_rows[1], weights[1], precision=exact_mode)
    imag_part = jnp.einsum(
        "vck,vn->nck", band_rows[0], weights[1], precision=exact_mode
    ) + jnp.einsum("vck,vn->nck", band_rows[1], weights[0], precision=exact_mode)
    return jnp.stack([real_part, imag_part])


def column_transform(coefficients, phase_grid):
    mixed_cols = jnp.einsum("pbck,pqkz->qbzc", coefficients, phase_grid, precision=exact_mode)
    return lax.all_to_all(mixed_cols, "pw", split_axis=2, concat_axis=3, tiled=True)


def to_grid(columns, inverse_map, phase_grid, grid_len):
    item_rows = columns.shape[1]
    col_count = columns.shape[2]
    rows_first = columns.reshape(2 * item_rows, col_count).T
    padded = jnp.concatenate([rows_first, jnp.zeros((1, 2 * item_rows), jnp.float32)], axis=0)
    placed = jnp.take(padded, inverse_map, axis=0)
    field_grid = placed.T.reshape(2, item_rows, grid_len, grid_len)
    field_grid = jnp.einsum("pzxk,pqky->qzxy", field_grid, phase_grid, precision=exact_mode)
    return jnp.einsum("pzky,pqkx->qzxy", field_grid, phase_grid, precision=exact_mode)


def from_grid(field_grid, column_map, phase_grid, grid_len):
    item_rows = field_grid.shape[1]
    field_grid = jnp.einsum("pzxk,pqky->qzxy", field_grid, phase_grid, precision=exact_mode)
    field_grid = jnp.einsum("pzky,pqkx->qzxy", field_grid, phase_grid, precision=exact_mode)
    cells_first = field_grid.reshape(2 * item_rows, grid_len * grid_len).T
    picked = jnp.take(cells_first, column_map, axis=0)
    return picked.T.reshape(2, item_rows, column_map.shape[0])


def on_device(
    occupied_bands,
    iterate,
    residual,
    old_direction,
    preconditioner,
    old_norm,
    eigenvalues,
    band_slot,
    potential,
    column_map,
):
    grid_len = potential.shape[1]
    planes = potential.shape[0]
    local_bands = iterate.shape[1]
    local_cols = iterate.shape[2]
    col_count = column_map.shape[0]
    total_pw = col_count * grid_len
    forward_table = phase_table(grid_len, 1.0)
    inverse_table = phase_table(grid_len, -1.0)
    inverse_map = (
        jnp.full((grid_len * grid_len,), col_count, jnp.int32)
        .at[column_map]
        .set(jnp.arange(col_count, dtype=jnp.int32))
    )
    my_columns = lax.dynamic_slice_in_dim(column_map, lax.axis_index("pw") * local_cols, local_cols)
    squares = wave_squares(my_columns, grid_len)
    kinetic = squares.astype(jnp.float32) * (4.0 / (grid_len * grid_len))
    sphere = (squares < grid_len // 4 * (grid_len // 4)).astype(jnp.float32)
    occupied = occupied_bands * sphere
    start_wave = iterate * sphere
    masked_residual = residual * sphere
    previous = old_direction * sphere
    weight = preconditioner * sphere
    owner_ids = lax.dynamic_slice_in_dim(
        band_slot, lax.axis_index("band") * local_bands, local_bands
    )
    select = (
        owner_ids[:, None] == jnp.arange(band_slot.shape[0], dtype=jnp.int32)[None, :]
    ).astype(jnp.float32)
    band_energy = jnp.dot(select, eigenvalues, precision=exact_mode)
    all_occupied = lax.all_gather(occupied_bands, "band", axis=1, tiled=True) * sphere
    smoothed = weight[None] * masked_residual
    norm_local = (
        jnp.sum(weight[None] * masked_residual * masked_residual, axis=(0, 2, 3)) / total_pw
    )
    new_norm = lax.psum(norm_local, "pw")
    beta_ratio = new_norm / old_norm
    direction = smoothed + beta_ratio[None, :, None, None] * previous
    weights = lax.psum(correlation(all_occupied, direction), "pw")
    projected = expand(all_occupied, weights)
    direction_cols = column_transform(direction, forward_table)
    field_grid = to_grid(
        direction_cols.reshape(2, local_bands * planes, -1), inverse_map, forward_table, grid_len
    )
    field_grid = (
        field_grid.reshape(2, local_bands, planes, grid_len, grid_len) * potential[None, None]
    ).reshape(2, local_bands * planes, grid_len, grid_len)
    returned = from_grid(field_grid, column_map, inverse_table, grid_len)
    gathered_back = lax.all_to_all(
        returned.reshape(2, local_bands, planes, -1), "pw", split_axis=3, concat_axis=2, tiled=True
    )
    local_potential = jnp.einsum(
        "pbzc,pqzk->qbck", gathered_back, inverse_table, precision=exact_mode
    ) / float(grid_len**3)
    applied = (
        local_potential * sphere
        + (kinetic[None, None] - band_energy[None, :, None, None]) * direction
        + projected
    )
    curvature_local = jnp.sum(direction * applied, axis=(0, 2, 3)) / total_pw
    curvature = lax.psum(curvature_local, "pw")
    step_size = new_norm / curvature
    new_iterate = start_wave + step_size[None, :, None, None] * direction
    new_residual = masked_residual - step_size[None, :, None, None] * applied
    joined = column_transform(jnp.concatenate([occupied, new_iterate], axis=1), forward_table)
    both_grids = to_grid(
        joined.reshape(2, 2 * local_bands * planes, -1), inverse_map, forward_table, grid_len
    )
    both_grids = both_grids.reshape(2, 2, local_bands, planes, grid_len, grid_len)
    density_local = jnp.sum(both_grids[:, 0] * both_grids[:, 1], axis=(0, 1)) * (4.0 / total_pw)
    density = lax.psum_scatter(density_local, "band", scatter_dimension=1, tiled=True)
    return (new_iterate, new_residual, direction, new_norm, density)


def solution(mesh):
    in_specs = (
        P(None, "band", "pw", None),
        P(None, "band", "pw", None),
        P(None, "band", "pw", None),
        P(None, "band", "pw", None),
        P("band", "pw", None),
        P("band"),
        P(),
        P(),
        P("pw", None, None),
        P(),
    )
    out_specs = (
        P(None, "band", "pw", None),
        P(None, "band", "pw", None),
        P(None, "band", "pw", None),
        P("band"),
        P("pw", "band", None),
    )
    return jax.shard_map(
        on_device, mesh=mesh, in_specs=in_specs, out_specs=out_specs, check_vma=False
    )
```

profile of v0, /device:TPU:4, one launch (start us, length us, event | category | flops | bytes accessed | tf_op | source)
XLA Modules:
  0.0 811.0 jit_solution(9233818517082111334)
XLA Ops:
  7.8 0.8 fusion.64
  8.6 0.9 broadcast_multiply_fusion.2
  9.5 1.6 copy_multiply_fusion.1
  11.4 145.6 %psum.21 = f32[2]{0:T(128)S(1)} all-reduce(f32[2]{0:T(128)S(1)} %broadcast_multiply_fusion.4), channel_id=1, replica_groups=mesh['band'=8,'pw'=64] {'pw'}, use_global_device_ids=true, to_apply=%region_1.2 | all-reduce | flops 2 | bytes 16 | tf_op jit(solution)/shard_map/psum | solution.py:119
  157.0 0.7 div.31
  157.6 1.0 multiply_add_fusion
  158.7 0.8 fusion.33
  159.5 0.6 copy-done.2
  160.6 1.2 reshape.312
  161.9 11.0 %all-to-all-start = ((f32[64,1,416]{2,1,0:T(1,128)}), f32[64,1,416]{2,1,0:T(1,128)S(1)}, u32[]{:S(2)}, u32[]{:S(2)}) async-start(f32[64,1,416]{2,1,0:T(1,128)} %reshape.312), calls=%async_computation | async-start | bytes 262144 | tf_op jit(solution)/shard_map/all_to_all | solution.py:50
  172.8 0.7 compare_select_fusion.1
  173.5 0.7 compare_and_fusion.1
  174.3 1.0 copy.102
  175.2 14.0 %all_gather.3 = f32[2,16,52,128]{3,0,2,1:T(2,128)S(1)} all-gather(f32[2,2,52,128]{3,0,2,1:T(2,128)S(1)} %copy.102), channel_id=1, replica_groups=mesh['band'=8,'pw'=64] {'band'}, dimensions={1}, use_global_device_ids=true | all-gather | bytes 958464 | tf_op jit(solution)/shard_map/all_gather | solution.py:114
  189.4 1.1 convolution_bitcast_fusion.7
  190.6 0.6 convolution_bitcast_fusion.9
  191.2 0.6 fusion.6
  191.8 138.8 %psum.22 = f32[2,16,2]{1,2,0:T(2,128)S(1)} all-reduce(f32[2,16,2]{1,2,0:T(2,128)S(1)} %pad_maximum_fusion.12), channel_id=1, replica_groups=mesh['band'=8,'pw'=64] {'pw'}, use_global_device_ids=true, to_apply=%region_3.4 | all-reduce | flops 64 | bytes 512 | tf_op jit(solution)/shard_map/psum | solution.py:122
  330.6 1.0 fusion.15
  331.6 1.0 fusion.17
  332.5 1.0 fusion.14
  333.5 1.0 fusion.16
  334.5 0.7 fusion.57
  335.2 0.6 pad_clamp_fusion
  335.8 12.7 %scatter_custom_fusion = s32[16384]{0:T(1024)S(1)} fusion(s32[3328]{0:T(1024)S(1)} %compare_select_fusion.1, s32[3328]{0:T(1024)S(1)} %iota.54, s32[]{:T(128)} %constant.107.clone.1), kind=kCustom, calls=%fused_computation.104 | custom fusion | bytes 65540 | tf_op jit(solution)/shard_map/scatter | solution.py:96
  348.5 0.6 fusion.49
  349.4 0.6 compare_and_fusion
  350.1 0.6 broadcast.378
  350.7 1.0 reduce.1
  353.0 60.2 %gather_fusion = f32[16384,8]{1,0:T(8,128)} fusion(f32[3329,8]{1,0:T(8,128)S(1)} %concatenate.9, s32[16384]{0:T(1024)} %fusion.49), kind=kCustom, calls=%fused_computation | custom fusion | bytes 1114112 | tf_op jit(solution)/shard_map/jit(_take)/gather | solution.py:58
  413.2 13.1 %select_bitcast_fusion.1 = f32[8,16384]{0,1:T(8,128)} fusion(f32[16384,8]{1,0:T(8,128)} %gather_fusion, pred[16384]{0:T(1024)(128)(4,1)S(1)} %copy-done.24), kind=kLoop, calls=%fused_computation.5 | loop fusion | flops 131072 | bytes 1064960 | tf_op jit(solution)/shard_map/jit(_take)/select_n | solution.py:58
  426.3 5.6 copy.86
  432.1 1.1 convolution_bitcast_fusion.3
  433.2 1.1 fusion.1
  434.3 1.1 convolution_bitcast_fusion.1
  435.4 1.1 fusion.26
  436.8 5.3 copy.95
  442.0 8.8 %gather_fusion.1 = f32[3328,8]{1,0:T(8,128)S(1)} fusion(f32[16384,8]{1,0:T(8,128)} %bitcast.224, s32[4096]{0:T(1024)S(1)} %copy-done.30), kind=kCustom, calls=%fused_computation.1 | custom fusion | bytes 226304 | tf_op jit(solution)/shard_map/jit(_take)/gather | solution.py:69
  450.9 1.7 select_bitcast_fusion.2
  452.7 6.6 reshape.309
  459.3 10.1 %reshape.314 = f32[64,1,416]{2,1,0:T(1,128)} reshape(f32[3328,2,2,2]{3,2,1,0:T(2,128)} %bitcast.226) | data formatting | bytes 212992
  469.4 14.6 %all-to-all-start.1 = ((f32[64,1,416]{2,1,0:T(1,128)}), f32[64,1,416]{2,1,0:T(1,128)S(1)}, u32[]{:S(2)}, u32[]{:S(2)}) async-start(f32[64,1,416]{2,1,0:T(1,128)} %reshape.314), calls=%async_computation.1 | async-start | bytes 262144 | tf_op jit(solution)/shard_map/all_to_all | solution.py:132
  484.3 14.1 %all-to-all-done.1 = f32[64,1,416]{2,1,0:T(1,128)S(1)} async-done(((f32[64,1,416]{2,1,0:T(1,128)}), f32[64,1,416]{2,1,0:T(1,128)S(1)}, u32[]{:S(2)}, u32[]{:S(2)}) %all-to-all-start.1) | async-done | bytes 106528 | tf_op jit(solution)/shard_map/all_to_all | solution.py:132
  498.4 1.0 reduce.2
  499.4 11.8 %reshape.315 = f32[3328,2,2,2]{3,2,1,0:T(2,128)} reshape(f32[64,416]{1,0:T(8,128)S(1)} %reduce.2) | data formatting | bytes 212992
  511.2 10.3 %copy.165 = f32[2,2,2,64,52]{4,3,2,1,0:T(8,128)S(1)} copy(f32[2,2,2,64,52]{2,1,0,4,3:T(2,128)} %bitcast.225) | data formatting | bytes 212992 | tf_op jit(solution)/shard_map/all_to_all | solution.py:132
  521.7 0.7 multiply_reduce_fusion
  522.4 136.6 %psum.23 = f32[2]{0:T(128)S(1)} all-reduce(f32[2]{0:T(128)S(1)} %broadcast_multiply_fusion.3), channel_id=1, replica_groups=mesh['band'=8,'pw'=64] {'pw'}, use_global_device_ids=true, to_apply=%region_5.6 | all-reduce | flops 2 | bytes 16 | tf_op jit(solution)/shard_map/psum | solution.py:144
  659.1 0.7 multiply_subtract_fusion
  659.8 0.6 copy-done.15
  661.1 0.9 reshape.316
  662.0 26.3 %all_to_all.48 = f32[64,1,832]{2,1,0:T(1,128)S(1)} all-to-all(f32[64,1,832]{2,1,0:T(1,128)S(1)} %reshape.316), channel_id=1, replica_groups=mesh['band'=8,'pw'=64] {'pw'}, dimensions={0} | all-to-all | bytes 425984 | tf_op jit(solution)/shard_map/all_to_all | solution.py:50
  688.3 1.2 reduce.3
  689.6 0.9 reshape.317
  691.5 60.0 %gather_fusion.2 = f32[16384,16]{1,0:T(8,128)} fusion(f32[3329,16]{1,0:T(8,128)S(1)} %concatenate.11, s32[16384]{0:T(1024)} %fusion.49), kind=kCustom, calls=%fused_computation.2 | custom fusion | bytes 2162688 | tf_op jit(solution)/shard_map/jit(_take)/gather | solution.py:58
  751.5 13.2 %select_bitcast_fusion = f32[16,16384]{0,1:T(8,128)} fusion(f32[16384,16]{1,0:T(8,128)} %gather_fusion.2, pred[16384]{0:T(1024)(128)(4,1)S(1)} %copy-done.25), kind=kLoop, calls=%fused_computation.4 | loop fusion | flops 262144 | bytes 2113536 | tf_op jit(solution)/shard_map/jit(_take)/select_n | solution.py:58
  764.7 5.2 copy.118
  769.8 2.0 convolution_bitcast_fusion
  771.8 1.9 fusion.20
  773.8 0.7 broadcast_multiply_fusion
  774.5 0.7 copy.125
  775.2 0.7 copy.123
  775.9 0.7 copy.124
  776.6 27.5 %reduce-scatter.2.cloned.1.call-done = f32[2,16,128]{2,1,0:T(8,128)} async-done(((f32[2,128,128]{2,1,0:T(8,128)}), f32[2,16,128]{2,1,0:T(8,128)}) %reduce-scatter.2.cloned.1.call-update) | async-done | bytes 16400 | tf_op jit(solution)/shard_map/reduce_scatter | solution.py:154
  (106 shorter events, 5.8 us)
Async XLA Ops:
  7.2 342.1 %copy-start = (f32[16]{0:T(128)S(1)}, f32[16]{0:T(128)}, u32[]{:S(2)}) copy-start(f32[16]{0:T(128)} %param.16) | copy-start | bytes 196
  7.2 342.0 %copy-start.31 = (s32[16]{0:T(128)S(1)}, s32[16]{0:T(128)}, u32[]{:S(2)}) copy-start(s32[16]{0:T(128)} %param.17) | copy-start | bytes 196
  8.6 343.6 %copy-start.13 = (f32[52,128]{1,0:T(8,128)}, f32[52,128]{1,0:T(8,128)S(1)}, u32[]{:S(2)}) copy-start(f32[52,128]{1,0:T(8,128)S(1)} %fusion.58) | copy-start | bytes 79876
  157.0 4.9 copy-start.32
  158.7 194.2 %copy-start.6 = (f32[2,2,52,128]{3,2,1,0:T(8,128)}, f32[2,2,52,128]{3,2,1,0:T(8,128)S(1)}, u32[]{:S(2)}) copy-start(f32[2,2,52,128]{3,2,1,0:T(8,128)S(1)} %multiply_add_fusion) | copy-start | bytes 319492
  159.4 0.7 copy-start.2
  161.9 188.2 %all-to-all-start = ((f32[64,1,416]{2,1,0:T(1,128)}), f32[64,1,416]{2,1,0:T(1,128)S(1)}, u32[]{:S(2)}, u32[]{:S(2)}) async-start(f32[64,1,416]{2,1,0:T(1,128)} %reshape.312), calls=%async_computation | async-start | bytes 262144 | tf_op jit(solution)/shard_map/all_to_all | solution.py:50
  353.0 60.2 %copy-start.24 = (pred[16384]{0:T(1024)(128)(4,1)S(1)}, pred[16384]{0:T(1024)(128)(4,1)}, u32[]{:S(2)}) copy-start(pred[16384]{0:T(1024)(128)(4,1)} %compare_and_fusion) | copy-start | bytes 49156
  426.3 5.8 copy-start.3
  426.3 6.8 copy-start.26
  426.3 7.9 copy-start.9
  426.3 8.0 copy-start.11
  432.0 10.1 %copy-start.30 = (s32[4096]{0:T(1024)S(1)}, s32[4096]{0:T(1024)}, u32[]{:S(2)}) copy-start(s32[4096]{0:T(1024)} %pad_clamp_fusion) | copy-start | bytes 49156
  452.6 31.5 %copy-start.28 = (f32[52,128]{1,0:T(8,128)S(1)}, f32[52,128]{1,0:T(8,128)}, u32[]{:S(2)}) copy-start(f32[52,128]{1,0:T(8,128)} %get-tuple-element.31) | copy-start | bytes 79876
  452.6 31.6 %copy-start.20 = (f32[2,52,128]{2,0,1:T(2,128)S(1)}, f32[2,52,128]{2,0,1:T(2,128)}, u32[]{:S(2)}) copy-start(f32[2,52,128]{2,0,1:T(2,128)} %fusion.15) | copy-start | bytes 159748
  452.6 31.6 %copy-start.21 = (f32[2,52,128]{2,0,1:T(2,128)S(1)}, f32[2,52,128]{2,0,1:T(2,128)}, u32[]{:S(2)}) copy-start(f32[2,52,128]{2,0,1:T(2,128)} %fusion.17) | copy-start | bytes 159748
  452.6 31.5 %copy-start.22 = (f32[2,52,128]{2,0,1:T(2,128)S(1)}, f32[2,52,128]{2,0,1:T(2,128)}, u32[]{:S(2)}) copy-start(f32[2,52,128]{2,0,1:T(2,128)} %fusion.14) | copy-start | bytes 159748
  452.7 31.5 %copy-start.23 = (f32[2,52,128]{2,0,1:T(2,128)S(1)}, f32[2,52,128]{2,0,1:T(2,128)}, u32[]{:S(2)}) copy-start(f32[2,52,128]{2,0,1:T(2,128)} %fusion.16) | copy-start | bytes 159748
  469.4 52.3 %copy-start.7 = (f32[2,2,52,128]{3,2,1,0:T(8,128)S(1)}, f32[2,2,52,128]{3,2,1,0:T(8,128)}, u32[]{:S(2)}) copy-start(f32[2,2,52,128]{3,2,1,0:T(8,128)} %copy-done.6) | copy-start | bytes 319492
  469.4 52.3 %copy-start.10 = (f32[1,2,128,128]{3,2,1,0:T(8,128)S(1)}, f32[1,2,128,128]{3,2,1,0:T(8,128)}, u32[]{:S(2)}) copy-start(f32[1,2,128,128]{3,2,1,0:T(8,128)} %get-tuple-element.22) | copy-start | bytes 393220
  469.4 52.3 %copy-start.12 = (f32[1,2,128,128]{3,2,1,0:T(8,128)S(1)}, f32[1,2,128,128]{3,2,1,0:T(8,128)}, u32[]{:S(2)}) copy-start(f32[1,2,128,128]{3,2,1,0:T(8,128)} %get-tuple-element.25) | copy-start | bytes 393220
  469.4 52.3 %copy-start.27 = (f32[52,128]{1,0:T(8,128)S(1)}, f32[52,128]{1,0:T(8,128)}, u32[]{:S(2)}) copy-start(f32[52,128]{1,0:T(8,128)} %get-tuple-element.30) | copy-start | bytes 79876
  469.4 189.7 %copy-start.33 = (f32[2]{0:T(128)S(1)}, f32[2]{0:T(128)}, u32[]{:S(2)}) copy-start(f32[2]{0:T(128)} %copy-done.32) | copy-start | bytes 28
  469.4 189.6 %copy-start.14 = (f32[52,128]{1,0:T(8,128)S(1)}, f32[52,128]{1,0:T(8,128)}, u32[]{:S(2)}) copy-start(f32[52,128]{1,0:T(8,128)} %copy-done.13) | copy-start | bytes 79876
  469.4 189.6 %copy-start.17 = (f32[2,2,52,128]{3,1,2,0:T(2,128)S(1)}, f32[2,2,52,128]{3,1,2,0:T(2,128)}, u32[]{:S(2)}) copy-start(f32[2,2,52,128]{3,1,2,0:T(2,128)} %param.12) | copy-start | bytes 319492
  469.4 189.6 %copy-start.29 = (f32[2,2,52,128]{3,1,2,0:T(2,128)S(1)}, f32[2,2,52,128]{3,1,2,0:T(2,128)}, u32[]{:S(2)}) copy-start(f32[2,2,52,128]{3,1,2,0:T(2,128)} %param.11) | copy-start | bytes 319492
  469.4 29.0 %all-to-all-start.1 = ((f32[64,1,416]{2,1,0:T(1,128)}), f32[64,1,416]{2,1,0:T(1,128)S(1)}, u32[]{:S(2)}, u32[]{:S(2)}) async-start(f32[64,1,416]{2,1,0:T(1,128)} %reshape.314), calls=%async_computation.1 | async-start | bytes 262144 | tf_op jit(solution)/shard_map/all_to_all | solution.py:132
  484.0 320.1 %reduce-scatter.2.cloned.1.call-start = ((), (), s32[]{:S(2)}) async-start(), calls=%async_computation.4 | async-start | bytes 147456 | tf_op jit(solution)/shard_map/reduce_scatter | solution.py:154
  484.2 176.2 %copy-start.4 = (f32[1,2,128,128]{3,2,0,1:T(8,128)S(1)}, f32[1,2,128,128]{3,2,0,1:T(8,128)}, u32[]{:S(2)}) copy-start(f32[1,2,128,128]{3,2,0,1:T(8,128)} %copy-done.2) | copy-start | bytes 393220
  484.2 176.2 %copy-start.19 = (f32[2,2,52,128]{3,2,1,0:T(8,128)S(1)}, f32[2,2,52,128]{3,2,1,0:T(8,128)}, u32[]{:S(2)}) copy-start(f32[2,2,52,128]{3,2,1,0:T(8,128)} %get-tuple-element.28) | copy-start | bytes 319492
  659.8 0.6 copy-start.15
  691.5 60.0 %copy-start.25 = (pred[16384]{0:T(1024)(128)(4,1)S(1)}, pred[16384]{0:T(1024)(128)(4,1)}, u32[]{:S(2)}) copy-start(pred[16384]{0:T(1024)(128)(4,1)} %compare_and_fusion) | copy-start | bytes 49156
  751.5 52.6 %copy-start.1 = (f32[16]{0:T(128)S(1)}, f32[16]{0:T(128)}, u32[]{:S(2)}) copy-start(f32[16]{0:T(128)} %param.16) | copy-start | bytes 196
  764.7 5.2 copy-start.5
  764.7 9.8 %copy-start.8 = (f32[2,2,52,128]{3,2,1,0:T(8,128)S(1)}, f32[2,2,52,128]{3,2,1,0:T(8,128)}, u32[]{:S(2)}) copy-start(f32[2,2,52,128]{3,2,1,0:T(8,128)} %copy-done.6) | copy-start | bytes 319492
  764.7 10.5 %copy-start.16 = (f32[2,2,52,128]{3,2,1,0:T(8,128)S(1)}, f32[2,2,52,128]{3,2,1,0:T(8,128)}, u32[]{:S(2)}) copy-start(f32[2,2,52,128]{3,2,1,0:T(8,128)} %copy-done.15) | copy-start | bytes 319492
  764.7 11.2 %copy-start.18 = (f32[2,2,52,128]{3,2,1,0:T(8,128)S(1)}, f32[2,2,52,128]{3,2,1,0:T(8,128)}, u32[]{:S(2)}) copy-start(f32[2,2,52,128]{3,2,1,0:T(8,128)} %get-tuple-element.26) | copy-start | bytes 319492
Sparse Core Ops, SparseCore 0:
  774.6 29.4 reduce-scatter.1
where the time goes:
time: 815 us; the launch traced here: 811 us
  blocking collectives  461 us (57%)
  local copies, waits for them, and re-layouts  208 us (26%)
  other arithmetic  43.7 us (5%)
  waiting for transfers between devices  41.7 us (5%)
  starting transfers between devices  25.6 us (3%)
  matrix products  15.8 us (2%)
  between operations  14.7 us (2%)
    psum x1, blocking collectives, on_device(): new_norm = lax.psum(norm_local, 'pw')  146 us
    psum x1, blocking collectives, on_device(): weights = lax.psum(correlation(all_occupied, direction), 'pw')  139 us
    psum x1, blocking collectives, on_device(): curvature = lax.psum(curvature_local, 'pw')  137 us
    gather x2, local copies, waits for them, and re-layouts, to_grid(): placed = jnp.take(padded, inverse_map, axis=0)  120 us
    unnamed x80, local copies, waits for them, and re-layouts  30.2 us
    reduce_scatter x1, waiting for transfers between devices, on_device(): lax.psum_scatter(density_local, 'band', scatter_dimension=1, tiled=True)  27.5 us
    all_to_all x1, blocking collectives, column_transform(): lax.all_to_all(mixed_cols, 'pw', split_axis=2, concat_axis=3, tiled=True)  26.3 us
    select_n x2, other arithmetic, to_grid(): placed = jnp.take(padded, inverse_map, axis=0)  26.3 us
  transfers between devices with their start and end apart: 3, of which 2 were waited for; matrix products, arithmetic and copies ran while one was open for 3% of the time, Pallas kernels for 0%

commit v1 on v0

--- a/solution.py
+++ b/solution.py
@@ -119,7 +119,7 @@
     new_norm = lax.psum(norm_local, "pw")
     beta_ratio = new_norm / old_norm
     direction = smoothed + beta_ratio[None, :, None, None] * previous
-    weights = lax.psum(correlation(all_occupied, direction), "pw")
+    weights = jnp.sum(lax.all_gather(correlation(all_occupied, direction), "pw"), axis=0)
     projected = expand(all_occupied, weights)
     direction_cols = column_transform(direction, forward_table)
     field_grid = to_grid(

time: 815 us -> 782 us (0.960)
  the two profiles are of different devices: /device:TPU:4 before, /device:TPU:2 now
where the time goes in v1:
time: 782 us; the launch traced here: 772 us
  blocking collectives  423 us (54%)
  local copies, waits for them, and re-layouts  208 us (27%)
  other arithmetic  43.7 us (6%)
  waiting for transfers between devices  42.1 us (5%)
  starting transfers between devices  23.9 us (3%)
  matrix products  15.8 us (2%)
  between operations  14.9 us (2%)
    psum x1, blocking collectives, on_device(): new_norm = lax.psum(norm_local, 'pw')  146 us
    psum x1, blocking collectives, on_device(): curvature = lax.psum(curvature_local, 'pw')  141 us
    gather x2, local copies, waits for them, and re-layouts, to_grid(): placed = jnp.take(padded, inverse_map, axis=0)  120 us
    all_gather x1, blocking collectives, on_device(): lax.all_gather(correlation(all_occupied, direction), 'pw')  99.9 us
    unnamed x80, local copies, waits for them, and re-layouts  30.2 us
    reduce_scatter x1, waiting for transfers between devices, on_device(): lax.psum_scatter(density_local, 'band', scatter_dimension=1, tiled=True)  27.2 us
    select_n x2, other arithmetic, to_grid(): placed = jnp.take(padded, inverse_map, axis=0)  26.3 us
    all_to_all x1, blocking collectives, column_transform(): lax.all_to_all(mixed_cols, 'pw', split_axis=2, concat_axis=3, tiled=True)  22.6 us
  transfers between devices with their start and end apart: 3, of which 2 were waited for; matrix products, arithmetic and copies ran while one was open for 3% of the time, Pallas kernels for 0%

profile of v1, /device:TPU:2, one launch (start us, length us, event | category | flops | bytes accessed | tf_op | source)
XLA Modules:
  0.0 771.8 jit_solution(13776496611948767670)
XLA Ops:
  7.8 0.8 fusion.64
  8.6 0.9 broadcast_multiply_fusion.2
  9.5 1.6 copy_multiply_fusion.1
  11.4 145.7 %psum.14 = f32[2]{0:T(128)S(1)} all-reduce(f32[2]{0:T(128)S(1)} %broadcast_multiply_fusion.4), channel_id=1, replica_groups=mesh['band'=8,'pw'=64] {'pw'}, use_global_device_ids=true, to_apply=%region_1.2 | all-reduce | flops 2 | bytes 16 | tf_op jit(solution)/shard_map/psum | solution.py:119
  157.1 0.7 div.31
  157.7 1.0 multiply_add_fusion
  158.8 0.8 fusion.33
  159.5 0.6 copy-done.2
  160.7 1.2 reshape.313
  162.0 10.9 %all-to-all-start = ((f32[64,1,416]{2,1,0:T(1,128)}), f32[64,1,416]{2,1,0:T(1,128)S(1)}, u32[]{:S(2)}, u32[]{:S(2)}) async-start(f32[64,1,416]{2,1,0:T(1,128)} %reshape.313), calls=%async_computation | async-start | bytes 262144 | tf_op jit(solution)/shard_map/all_to_all | solution.py:50
  172.9 0.7 compare_select_fusion.1
  173.6 0.7 compare_and_fusion.1
  174.3 1.0 copy.102
  175.3 14.0 %all_gather.9 = f32[2,16,52,128]{3,0,2,1:T(2,128)S(1)} all-gather(f32[2,2,52,128]{3,0,2,1:T(2,128)S(1)} %copy.102), channel_id=1, replica_groups=mesh['band'=8,'pw'=64] {'band'}, dimensions={1}, use_global_device_ids=true | all-gather | bytes 958464 | tf_op jit(solution)/shard_map/all_gather | solution.py:114
  189.5 1.1 convolution_bitcast_fusion.7
  190.6 0.6 convolution_bitcast_fusion.9
  191.2 0.6 fusion.6
  191.8 99.9 %all-gather = f32[128,16,2]{1,2,0:T(2,128)S(1)} all-gather(f32[2,16,2]{1,2,0:T(2,128)S(1)} %pad_maximum_fusion.12), channel_id=2, replica_groups=mesh['band'=8,'pw'=64] {'pw'}, dimensions={0}, use_global_device_ids=true | all-gather | bytes 16640 | tf_op jit(solution)/shard_map/all_gather | solution.py:122
  291.8 1.0 fusion.15
  292.7 1.0 fusion.17
  293.7 1.0 fusion.14
  294.7 1.0 fusion.16
  295.6 0.7 fusion.57
  296.3 0.6 pad_clamp_fusion
  296.9 12.7 %scatter_custom_fusion = s32[16384]{0:T(1024)S(1)} fusion(s32[3328]{0:T(1024)S(1)} %compare_select_fusion.1, s32[3328]{0:T(1024)S(1)} %iota.54, s32[]{:T(128)} %constant.107.clone.1), kind=kCustom, calls=%fused_computation.104 | custom fusion | bytes 65540 | tf_op jit(solution)/shard_map/scatter | solution.py:96
  309.7 0.6 fusion.49
  310.6 0.6 compare_and_fusion
  311.2 0.6 broadcast.378
  311.8 1.0 reduce.1
  314.2 60.4 %gather_fusion = f32[16384,8]{1,0:T(8,128)} fusion(f32[3329,8]{1,0:T(8,128)S(1)} %concatenate.9, s32[16384]{0:T(1024)} %fusion.49), kind=kCustom, calls=%fused_computation | custom fusion | bytes 1114112 | tf_op jit(solution)/shard_map/jit(_take)/gather | solution.py:58
  374.6 13.1 %select_bitcast_fusion.1 = f32[8,16384]{0,1:T(8,128)} fusion(f32[16384,8]{1,0:T(8,128)} %gather_fusion, pred[16384]{0:T(1024)(128)(4,1)S(1)} %copy-done.24), kind=kLoop, calls=%fused_computation.5 | loop fusion | flops 131072 | bytes 1064960 | tf_op jit(solution)/shard_map/jit(_take)/select_n | solution.py:58
  387.8 5.6 copy.86
  393.5 1.1 convolution_bitcast_fusion.3
  394.6 1.1 fusion.1
  395.7 1.1 convolution_bitcast_fusion.1
  396.8 1.1 fusion.26
  398.2 5.3 copy.95
  403.5 8.8 %gather_fusion.1 = f32[3328,8]{1,0:T(8,128)S(1)} fusion(f32[16384,8]{1,0:T(8,128)} %bitcast.225, s32[4096]{0:T(1024)S(1)} %copy-done.30), kind=kCustom, calls=%fused_computation.1 | custom fusion | bytes 226304 | tf_op jit(solution)/shard_map/jit(_take)/gather | solution.py:69
  412.3 1.7 select_bitcast_fusion.2
  414.1 6.6 reshape.310
  420.7 10.1 %reshape.315 = f32[64,1,416]{2,1,0:T(1,128)} reshape(f32[3328,2,2,2]{3,2,1,0:T(2,128)} %bitcast.227) | data formatting | bytes 212992
  430.9 12.9 %all-to-all-start.1 = ((f32[64,1,416]{2,1,0:T(1,128)}), f32[64,1,416]{2,1,0:T(1,128)S(1)}, u32[]{:S(2)}, u32[]{:S(2)}) async-start(f32[64,1,416]{2,1,0:T(1,128)} %reshape.315), calls=%async_computation.1 | async-start | bytes 262144 | tf_op jit(solution)/shard_map/all_to_all | solution.py:132
  444.0 14.9 %all-to-all-done.1 = f32[64,1,416]{2,1,0:T(1,128)S(1)} async-done(((f32[64,1,416]{2,1,0:T(1,128)}), f32[64,1,416]{2,1,0:T(1,128)S(1)}, u32[]{:S(2)}, u32[]{:S(2)}) %all-to-all-start.1) | async-done | bytes 106528 | tf_op jit(solution)/shard_map/all_to_all | solution.py:132
  458.9 1.0 reduce.2
  459.9 11.8 %reshape.316 = f32[3328,2,2,2]{3,2,1,0:T(2,128)} reshape(f32[64,416]{1,0:T(8,128)S(1)} %reduce.2) | data formatting | bytes 212992
  471.7 10.3 %copy.165 = f32[2,2,2,64,52]{4,3,2,1,0:T(8,128)S(1)} copy(f32[2,2,2,64,52]{2,1,0,4,3:T(2,128)} %bitcast.226) | data formatting | bytes 212992 | tf_op jit(solution)/shard_map/all_to_all | solution.py:132
  482.3 0.7 multiply_reduce_fusion
  482.9 140.8 %psum.15 = f32[2]{0:T(128)S(1)} all-reduce(f32[2]{0:T(128)S(1)} %broadcast_multiply_fusion.3), channel_id=1, replica_groups=mesh['band'=8,'pw'=64] {'pw'}, use_global_device_ids=true, to_apply=%region_5.6 | all-reduce | flops 2 | bytes 16 | tf_op jit(solution)/shard_map/psum | solution.py:144
  623.7 0.7 multiply_subtract_fusion
  624.5 0.6 copy-done.15
  625.8 0.9 reshape.317
  626.7 22.6 %all_to_all.48 = f32[64,1,832]{2,1,0:T(1,128)S(1)} all-to-all(f32[64,1,832]{2,1,0:T(1,128)S(1)} %reshape.317), channel_id=1, replica_groups=mesh['band'=8,'pw'=64] {'pw'}, dimensions={0} | all-to-all | bytes 425984 | tf_op jit(solution)/shard_map/all_to_all | solution.py:50
  649.3 1.2 reduce.3
  650.5 0.9 reshape.318
  652.5 60.0 %gather_fusion.2 = f32[16384,16]{1,0:T(8,128)} fusion(f32[3329,16]{1,0:T(8,128)S(1)} %concatenate.11, s32[16384]{0:T(1024)} %fusion.49), kind=kCustom, calls=%fused_computation.2 | custom fusion | bytes 2162688 | tf_op jit(solution)/shard_map/jit(_take)/gather | solution.py:58
  712.4 13.2 %select_bitcast_fusion = f32[16,16384]{0,1:T(8,128)} fusion(f32[16384,16]{1,0:T(8,128)} %gather_fusion.2, pred[16384]{0:T(1024)(128)(4,1)S(1)} %copy-done.25), kind=kLoop, calls=%fused_computation.4 | loop fusion | flops 262144 | bytes 2113536 | tf_op jit(solution)/shard_map/jit(_take)/select_n | solution.py:58
  725.6 5.2 copy.118
  730.8 2.0 convolution_bitcast_fusion
  732.8 1.9 fusion.20
  734.7 0.7 broadcast_multiply_fusion
  735.4 0.7 copy.125
  736.1 0.7 copy.123
  736.8 0.7 copy.124
  737.5 27.2 %reduce-scatter.2.cloned.1.call-done = f32[2,16,128]{2,1,0:T(8,128)} async-done(((f32[2,128,128]{2,1,0:T(8,128)}), f32[2,16,128]{2,1,0:T(8,128)}) %reduce-scatter.2.cloned.1.call-update) | async-done | bytes 16400 | tf_op jit(solution)/shard_map/reduce_scatter | solution.py:154
  (107 shorter events, 5.9 us)
Async XLA Ops:
  7.2 303.2 %copy-start = (f32[16]{0:T(128)S(1)}, f32[16]{0:T(128)}, u32[]{:S(2)}) copy-start(f32[16]{0:T(128)} %param.16) | copy-start | bytes 196
  7.2 303.1 %copy-start.31 = (s32[16]{0:T(128)S(1)}, s32[16]{0:T(128)}, u32[]{:S(2)}) copy-start(s32[16]{0:T(128)} %param.17) | copy-start | bytes 196
  8.6 304.7 %copy-start.13 = (f32[52,128]{1,0:T(8,128)}, f32[52,128]{1,0:T(8,128)S(1)}, u32[]{:S(2)}) copy-start(f32[52,128]{1,0:T(8,128)S(1)} %fusion.58) | copy-start | bytes 79876
  157.1 4.9 copy-start.32
  158.8 155.3 %copy-start.6 = (f32[2,2,52,128]{3,2,1,0:T(8,128)}, f32[2,2,52,128]{3,2,1,0:T(8,128)S(1)}, u32[]{:S(2)}) copy-start(f32[2,2,52,128]{3,2,1,0:T(8,128)S(1)} %multiply_add_fusion) | copy-start | bytes 319492
  159.5 0.7 copy-start.2
  162.0 149.3 %all-to-all-start = ((f32[64,1,416]{2,1,0:T(1,128)}), f32[64,1,416]{2,1,0:T(1,128)S(1)}, u32[]{:S(2)}, u32[]{:S(2)}) async-start(f32[64,1,416]{2,1,0:T(1,128)} %reshape.313), calls=%async_computation | async-start | bytes 262144 | tf_op jit(solution)/shard_map/all_to_all | solution.py:50
  314.2 60.5 %copy-start.24 = (pred[16384]{0:T(1024)(128)(4,1)S(1)}, pred[16384]{0:T(1024)(128)(4,1)}, u32[]{:S(2)}) copy-start(pred[16384]{0:T(1024)(128)(4,1)} %compare_and_fusion) | copy-start | bytes 49156
  387.8 5.8 copy-start.3
  387.8 6.8 copy-start.26
  387.8 7.9 %copy-start.9 = (f32[1,2,128,128]{3,2,1,0:T(8,128)S(1)}, f32[1,2,128,128]{3,2,1,0:T(8,128)}, u32[]{:S(2)}) copy-start(f32[1,2,128,128]{3,2,1,0:T(8,128)} %get-tuple-element.22) | copy-start | bytes 393220
  387.8 8.0 %copy-start.11 = (f32[1,2,128,128]{3,2,1,0:T(8,128)S(1)}, f32[1,2,128,128]{3,2,1,0:T(8,128)}, u32[]{:S(2)}) copy-start(f32[1,2,128,128]{3,2,1,0:T(8,128)} %get-tuple-element.25) | copy-start | bytes 393220
  393.4 10.1 %copy-start.30 = (s32[4096]{0:T(1024)S(1)}, s32[4096]{0:T(1024)}, u32[]{:S(2)}) copy-start(s32[4096]{0:T(1024)} %pad_clamp_fusion) | copy-start | bytes 49156
  414.0 29.8 %copy-start.28 = (f32[52,128]{1,0:T(8,128)S(1)}, f32[52,128]{1,0:T(8,128)}, u32[]{:S(2)}) copy-start(f32[52,128]{1,0:T(8,128)} %get-tuple-element.31) | copy-start | bytes 79876
  414.1 29.9 %copy-start.20 = (f32[2,52,128]{2,0,1:T(2,128)S(1)}, f32[2,52,128]{2,0,1:T(2,128)}, u32[]{:S(2)}) copy-start(f32[2,52,128]{2,0,1:T(2,128)} %fusion.15) | copy-start | bytes 159748
  414.1 29.9 %copy-start.21 = (f32[2,52,128]{2,0,1:T(2,128)S(1)}, f32[2,52,128]{2,0,1:T(2,128)}, u32[]{:S(2)}) copy-start(f32[2,52,128]{2,0,1:T(2,128)} %fusion.17) | copy-start | bytes 159748
  414.1 29.9 %copy-start.22 = (f32[2,52,128]{2,0,1:T(2,128)S(1)}, f32[2,52,128]{2,0,1:T(2,128)}, u32[]{:S(2)}) copy-start(f32[2,52,128]{2,0,1:T(2,128)} %fusion.14) | copy-start | bytes 159748
  414.1 29.9 %copy-start.23 = (f32[2,52,128]{2,0,1:T(2,128)S(1)}, f32[2,52,128]{2,0,1:T(2,128)}, u32[]{:S(2)}) copy-start(f32[2,52,128]{2,0,1:T(2,128)} %fusion.16) | copy-start | bytes 159748
  430.8 51.4 %copy-start.7 = (f32[2,2,52,128]{3,2,1,0:T(8,128)S(1)}, f32[2,2,52,128]{3,2,1,0:T(8,128)}, u32[]{:S(2)}) copy-start(f32[2,2,52,128]{3,2,1,0:T(8,128)} %copy-done.6) | copy-start | bytes 319492
  430.8 51.4 %copy-start.10 = (f32[1,2,128,128]{3,2,1,0:T(8,128)S(1)}, f32[1,2,128,128]{3,2,1,0:T(8,128)}, u32[]{:S(2)}) copy-start(f32[1,2,128,128]{3,2,1,0:T(8,128)} %get-tuple-element.22) | copy-start | bytes 393220
  430.8 51.4 %copy-start.12 = (f32[1,2,128,128]{3,2,1,0:T(8,128)S(1)}, f32[1,2,128,128]{3,2,1,0:T(8,128)}, u32[]{:S(2)}) copy-start(f32[1,2,128,128]{3,2,1,0:T(8,128)} %get-tuple-element.25) | copy-start | bytes 393220
  430.8 51.4 %copy-start.27 = (f32[52,128]{1,0:T(8,128)S(1)}, f32[52,128]{1,0:T(8,128)}, u32[]{:S(2)}) copy-start(f32[52,128]{1,0:T(8,128)} %get-tuple-element.30) | copy-start | bytes 79876
  430.8 192.9 %copy-start.33 = (f32[2]{0:T(128)S(1)}, f32[2]{0:T(128)}, u32[]{:S(2)}) copy-start(f32[2]{0:T(128)} %copy-done.32) | copy-start | bytes 28
  430.8 192.9 %copy-start.14 = (f32[52,128]{1,0:T(8,128)S(1)}, f32[52,128]{1,0:T(8,128)}, u32[]{:S(2)}) copy-start(f32[52,128]{1,0:T(8,128)} %copy-done.13) | copy-start | bytes 79876
  430.8 192.9 %copy-start.17 = (f32[2,2,52,128]{3,1,2,0:T(2,128)S(1)}, f32[2,2,52,128]{3,1,2,0:T(2,128)}, u32[]{:S(2)}) copy-start(f32[2,2,52,128]{3,1,2,0:T(2,128)} %param.12) | copy-start | bytes 319492
  430.9 192.9 %copy-start.29 = (f32[2,2,52,128]{3,1,2,0:T(2,128)S(1)}, f32[2,2,52,128]{3,1,2,0:T(2,128)}, u32[]{:S(2)}) copy-start(f32[2,2,52,128]{3,1,2,0:T(2,128)} %param.11) | copy-start | bytes 319492
  430.9 28.1 %all-to-all-start.1 = ((f32[64,1,416]{2,1,0:T(1,128)}), f32[64,1,416]{2,1,0:T(1,128)S(1)}, u32[]{:S(2)}, u32[]{:S(2)}) async-start(f32[64,1,416]{2,1,0:T(1,128)} %reshape.315), calls=%async_computation.1 | async-start | bytes 262144 | tf_op jit(solution)/shard_map/all_to_all | solution.py:132
  443.8 320.9 %reduce-scatter.2.cloned.1.call-start = ((), (), s32[]{:S(2)}) async-start(), calls=%async_computation.4 | async-start | bytes 147456 | tf_op jit(solution)/shard_map/reduce_scatter | solution.py:154
  444.0 181.1 %copy-start.4 = (f32[1,2,128,128]{3,2,0,1:T(8,128)S(1)}, f32[1,2,128,128]{3,2,0,1:T(8,128)}, u32[]{:S(2)}) copy-start(f32[1,2,128,128]{3,2,0,1:T(8,128)} %copy-done.2) | copy-start | bytes 393220
  444.0 181.1 %copy-start.19 = (f32[2,2,52,128]{3,2,1,0:T(8,128)S(1)}, f32[2,2,52,128]{3,2,1,0:T(8,128)}, u32[]{:S(2)}) copy-start(f32[2,2,52,128]{3,2,1,0:T(8,128)} %get-tuple-element.28) | copy-start | bytes 319492
  624.5 0.6 copy-start.15
  652.4 60.0 %copy-start.25 = (pred[16384]{0:T(1024)(128)(4,1)S(1)}, pred[16384]{0:T(1024)(128)(4,1)}, u32[]{:S(2)}) copy-start(pred[16384]{0:T(1024)(128)(4,1)} %compare_and_fusion) | copy-start | bytes 49156
  712.4 52.3 %copy-start.1 = (f32[16]{0:T(128)S(1)}, f32[16]{0:T(128)}, u32[]{:S(2)}) copy-start(f32[16]{0:T(128)} %param.16) | copy-start | bytes 196
  725.6 5.2 copy-start.5
  725.6 9.8 %copy-start.8 = (f32[2,2,52,128]{3,2,1,0:T(8,128)S(1)}, f32[2,2,52,128]{3,2,1,0:T(8,128)}, u32[]{:S(2)}) copy-start(f32[2,2,52,128]{3,2,1,0:T(8,128)} %copy-done.6) | copy-start | bytes 319492
  725.6 10.5 %copy-start.16 = (f32[2,2,52,128]{3,2,1,0:T(8,128)S(1)}, f32[2,2,52,128]{3,2,1,0:T(8,128)}, u32[]{:S(2)}) copy-start(f32[2,2,52,128]{3,2,1,0:T(8,128)} %copy-done.15) | copy-start | bytes 319492
  725.6 11.2 %copy-start.18 = (f32[2,2,52,128]{3,2,1,0:T(8,128)S(1)}, f32[2,2,52,128]{3,2,1,0:T(8,128)}, u32[]{:S(2)}) copy-start(f32[2,2,52,128]{3,2,1,0:T(8,128)} %get-tuple-element.26) | copy-start | bytes 319492
Sparse Core Ops, SparseCore 0:
  735.5 29.1 reduce-scatter.1
